TPU v7x, 512 devices: a whole 4x8x8 slice. The times are simulated.
512 devices in a mesh: group: 16 (over y, core), leaf: 32 (over z, x).
Axes of the slice: x: 4, y: 8, z: 8, core: 2. Of those that a mesh axis runs over, the one named last changes fastest.
Arguments:
- left_vectors: float32 [256, 128], replicated, may hold values from -6 to 6
- panel_vectors: bfloat16 [2, 256, 128], replicated, may hold values from -0.375 to 0.375
- panel_factors: float32 [2, 128, 128], replicated, may hold values from -0.5 to 0.5
- node_y: bfloat16 [16, 32, 9, 256, 256], P('group', 'leaf')
- node_t: float32 [16, 32, 9, 128, 256], P('group', 'leaf'), as said below
- leaf_v: bfloat16 [262144, 256], P(('group', 'leaf')), may hold values from -0.375 to 0.375
- leaf_t: float32 [16, 32, 256, 256], P('group', 'leaf'), may hold values from -0.1875 to 0.1875
- leaf_map: int32 [16, 32], P('group', 'leaf'), may hold values from 0 to 31, as said below
Outputs:
- eofs: bfloat16 [262144, 128], P(('group', 'leaf'))
Inputs may be any that keep to these rules, and one draw needn't show every extreme that they name: leaf_map[g, s] is the leaf index of the device of group g that holds leaf slot s; slots 2m and 2m + 1 name devices 2m and 2m + 1 in either order. Every device that a node of level l covers holds the same node_y[., ., l]; every device in the first half of the node's devices holds the same node_t[., ., l], and so does every device in the second half.
All inputs are finite; a program needn't handle non-finite values.
Results may differ from a plain program's by a relative error of at most 0.0045.
Values sent between devices are 32-bit elements; how exact they have to be, the bound alone decides.
No kernel may reach another device: no remote copies, remote signals or barrier semaphores. Data moves between devices by JAX's collectives and lax.ppermute only.
A program may use at most 64 MiB of HBM per device.

v0:
```python
import jax
import jax.numpy as jnp
from jax import lax
from jax.experimental import pallas as pl
from jax.experimental.pallas import tpu as pltpu
from jax.sharding import PartitionSpec as P


ANY = pl.BlockSpec(memory_space=pl.ANY)
VMEM = pl.BlockSpec(memory_space=pltpu.VMEM)
SMEM = pl.BlockSpec(memory_space=pltpu.SMEM)
SMALL = pltpu.CompilerParams(vmem_limit_bytes=8 << 20)
f32 = jnp.float32
bf16 = jnp.bfloat16


def halves(value):
    high = value.astype(bf16)
    low = (value - high.astype(f32)).astype(bf16)
    return high, low


def mul(left, right):
    return jnp.dot(left, right, preferred_element_type=f32)


def exact_times(exact, value):
    columns = value.shape[1]
    both = mul(exact, jnp.concatenate(halves(value), axis=1))
    return both[:, :columns] + both[:, columns:]


def split_times(high, low, value):
    columns = value.shape[1]
    value_high, value_low = halves(value)
    both = mul(high, jnp.concatenate([value_high, value_low], axis=1))
    return both[:, :columns] + both[:, columns:] + mul(low, value_high)


def ring_partner(place):
    return (place + 1) % 8 if place % 2 else (place - 1) % 8


def ring_outer(place):
    return (place & 1) == ((place >> 1) & 1)


def places():
    group = lax.axis_index("group")
    leaf = lax.axis_index("leaf")
    return group >> 1, group & 1, leaf >> 2, leaf & 3


def is_ahead(z):
    return z == 0


def ahead():
    return is_ahead(lax.axis_index("leaf") >> 2)


def pieces_kernel(node_t, y_send, z_send, seven, eight, three, sems):
    y, _, z, _ = places()
    y_level = jnp.where(ring_outer(y), 0, 1)
    z_level = jnp.where(ring_outer(z), 4, 5)
    copies = [
        pltpu.make_async_copy(node_t.at[0, 0, level], out, sems.at[i])
        for i, (level, out) in enumerate(
            [(y_level, y_send), (z_level, z_send), (7, seven), (8, eight), (3, three)]
        )
    ]
    for copy in copies:
        copy.start()
    for copy in copies:
        copy.wait()


def in_vmem(array):
    return pltpu.with_memory_space_constraint(array, pltpu.VMEM)


def pieces(node_t):
    shape = pltpu.VMEM((128, 256), f32)
    return pl.pallas_call(
        pieces_kernel,
        out_shape=(shape,) * 5,
        in_specs=[ANY],
        out_specs=(VMEM,) * 5,
        scratch_shapes=[pltpu.SemaphoreType.DMA((5,))],
        name="pieces",
        compiler_params=SMALL,
    )(node_t)


def join(own, received, level):
    def kernel(own, *refs):
        out = refs[-1]
        out[0] = own[0, 0, level]
        if len(refs) == 2:
            out[1] = refs[0][...]
        else:
            out[1] = jnp.where(ahead(), refs[0][...], refs[1][...])

    return pl.pallas_call(
        kernel,
        out_shape=pltpu.VMEM((2, 128, 256), f32),
        in_specs=[VMEM] * (1 + len(received)),
        out_specs=VMEM,
        compiler_params=SMALL,
    )(own, *[in_vmem(array) for array in received])


def place_rows(high_ref, low_ref, slot, bit, value):
    rows = pl.ds(pl.multiple_of(bit * 128, 128), 128)
    high, low = halves(value)
    high_ref[slot, rows] = high
    low_ref[slot, rows] = low


def tree_step(x_ref, high, low, reflect, lower):
    weighted = split_times(high, low, x_ref[...])

    @pl.when(lower == 1)
    def _():
        x_ref[...] = -exact_times(reflect[...], weighted)

    @pl.when(lower == 0)
    def _():
        x_ref[...] = x_ref[...] - weighted


def group_kernel(
    left, vectors, factors, node_y, own, y_got, y_late, y_pair, three, x_out,
    high_ref, low_ref,
):
    y, core, _, _ = places()
    outer = ring_outer(y)
    row = jnp.where(outer, 0, 1)
    bits = [(y >> 2) & 1, (y >> 1) & 1, y & 1, core]

    x = left[...]
    for panel in (1, 0):
        vector = vectors[panel]
        columns = x.shape[1]
        both = lax.dot_general(
            vector,
            jnp.concatenate(halves(x), axis=1),
            (((0,), (0,)), ((), ())),
            preferred_element_type=f32,
        )
        projected = both[:, :columns] + both[:, columns:]
        scaled = split_times(*halves(factors[panel]), projected)
        x = x - exact_times(vector, scaled)
    x_out[...] = x

    ring_bit = jnp.where(outer, bits[0], bits[1])
    pair_bit = jnp.where(outer, bits[1], bits[0])
    for i in range(4):
        place_rows(high_ref, low_ref, i, bits[i], own[0, 0, i])
    place_rows(high_ref, low_ref, row, 1 - ring_bit, jnp.where(ahead(), y_got[...], y_late[...]))
    place_rows(high_ref, low_ref, 1 - row, 1 - pair_bit, y_pair[1])
    place_rows(high_ref, low_ref, 2, 1 - bits[2], y_pair[0])
    place_rows(high_ref, low_ref, 3, 1 - bits[3], three[...])
    for i in range(4):
        tree_step(x_out, high_ref[i], low_ref[i], node_y.at[0, 0, i], bits[i])


def leaf_kernel(
    x_in, node_y, own, z_got, z_pair, seven, eight, eight_late, leaf_v, leaf_t, leaf_map, out,
    x_ref, high_ref, low_ref,
):
    _, _, z, x_place = places()
    outer = ring_outer(z)
    row = jnp.where(outer, 0, 1)
    bits = [(z >> 2) & 1, (z >> 1) & 1, z & 1, (x_place >> 1) & 1, x_place & 1]
    x_ref[...] = x_in[...]
    flipped = leaf_map[0, 0] != lax.axis_index("leaf")
    last = jnp.where(flipped, 1 - bits[4], bits[4])
    lows = bits[:4] + [last]
    ring_bit = jnp.where(outer, bits[0], bits[1])
    pair_bit = jnp.where(outer, bits[1], bits[0])
    for i in range(5):
        place_rows(high_ref, low_ref, i, bits[i], own[0, 0, 4 + i])
    place_rows(high_ref, low_ref, row, 1 - ring_bit, z_got[...])
    place_rows(high_ref, low_ref, 1 - row, 1 - pair_bit, z_pair[1])
    place_rows(high_ref, low_ref, 2, 1 - bits[2], z_pair[0])
    place_rows(high_ref, low_ref, 3, 1 - bits[3], seven[...])
    place_rows(high_ref, low_ref, 4, 1 - bits[4], jnp.where(ahead(), eight[...], eight_late[...]))
    for i in range(5):
        tree_step(x_ref, high_ref[i], low_ref[i], node_y.at[0, 0, 4 + i], lows[i])
    x = x_ref[...]
    projected = lax.dot_general(
        leaf_v[:256], x.astype(bf16), (((0,), (0,)), ((), ())), preferred_element_type=f32
    )
    solved = split_times(*halves(leaf_t[0, 0]), projected).astype(bf16)
    out[:256] = (x - mul(leaf_v[:256], solved)).astype(bf16)
    out[256:] = (-mul(leaf_v[256:], solved)).astype(bf16)


def exchange(block, partner, planes=None):
    pairs = []
    for g in range(16):
        for j in range(32):
            place = (g >> 1, g & 1, j >> 2, j & 3)
            if planes is None or planes(place[2]):
                y, core, z, x = partner(*place)
                pairs.append((g * 32 + j, (y * 2 + core) * 32 + z * 4 + x))
    return lax.ppermute(block, ("group", "leaf"), pairs)


def is_behind(z):
    return not is_ahead(z)


def body(left_vectors, panel_vectors, panel_factors, node_y, node_t, leaf_v, leaf_t, leaf_map):
    def y_ring(y, core, z, x):
        return ring_partner(y), core, z, x

    def z_ring(y, core, z, x):
        return y, core, ring_partner(z), x

    def y_next(y, core, z, x):
        return y ^ 1, core, z, x

    def z_next(y, core, z, x):
        return y, core, z ^ 1, x

    def x_far(y, core, z, x):
        return y, core, z, x ^ 3

    def x_next(y, core, z, x):
        return y, core, z, x ^ 1

    def other_core(y, core, z, x):
        return y, 1 - core, z, x

    y_send, z_send, seven, eight, three = pieces(pltpu.with_memory_space_constraint(node_t, pltpu.HBM))
    own, node_y, leaf_v, leaf_t = [in_vmem(array) for array in (node_t, node_y, leaf_v, leaf_t)]
    y_got = [exchange(y_send, y_ring, is_ahead)]
    eight_got = [exchange(eight, x_next, is_ahead)]
    z_got = exchange(z_send, z_ring)
    y_got.append(exchange(y_send, y_ring, is_behind))
    eight_got.append(exchange(eight, x_next, is_behind))
    three_got = exchange(three, other_core)
    y_pair = exchange(join(own, y_got, 2), y_next)
    z_pair = exchange(join(own, [z_got], 6), z_next)
    seven_got = exchange(seven, x_far)
    x = pl.pallas_call(
        group_kernel,
        out_shape=pltpu.VMEM((256, 128), f32),
        in_specs=[VMEM] * 9,
        out_specs=VMEM,
        scratch_shapes=[pltpu.VMEM((4, 256, 256), bf16)] * 2,
        name="group_kernel",
        compiler_params=SMALL,
    )(
        in_vmem(left_vectors), in_vmem(panel_vectors), in_vmem(panel_factors), node_y, own,
        *[in_vmem(array) for array in (*y_got, y_pair, three_got)],
    )
    return pl.pallas_call(
        leaf_kernel,
        out_shape=jax.ShapeDtypeStruct((512, 128), bf16),
        in_specs=[VMEM] * 10 + [SMEM],
        out_specs=VMEM,
        scratch_shapes=[pltpu.VMEM((256, 128), f32)] + [pltpu.VMEM((5, 256, 256), bf16)] * 2,
        name="leaf_kernel",
        compiler_params=SMALL,
    )(
        in_vmem(x), node_y, own, *[in_vmem(array) for array in (z_got, z_pair, seven_got, *eight_got)],
        leaf_v, leaf_t, leaf_map,
    )


def solution(mesh):
    return jax.shard_map(
        body,
        mesh=mesh,
        in_specs=(
            P(),
            P(),
            P(),
            P("group", "leaf", None, None, None),
            P("group", "leaf", None, None, None),
            P(("group", "leaf"), None),
            P("group", "leaf", None, None),
            P("group", "leaf"),
        ),
        out_specs=P(("group", "leaf"), None),
        check_vma=False,
    )
```

profile of v0, /device:TPU:16, one launch (start us, length us, event | category | flops | bytes accessed | tf_op | source)
XLA Modules:
  0.0 40.9 jit_solution(12752486232965916133)
XLA Ops:
  0.0 0.0 copy-start
  0.0 1.3 %pieces.1 = (f32[128,256]{1,0:T(8,128)S(1)}, f32[128,256]{1,0:T(8,128)S(1)}, f32[128,256]{1,0:T(8,128)S(1)}, f32[128,256]{1,0:T(8,128)S(1)}, f32[128,256]{1,0:T(8,128)S(1)}) custom-call(f32[1,1,9,128,256]{4,3,2,1,0:T(8,128)} %own.7), custom_call_target="tpu_custom_call" | custom-call | tf_op jit(solution)/shard_map/pieces/pallas_call | solution.py:84
  1.3 2.4 %collective-permute-start = (f32[128,256]{1,0:T(8,128)S(1)}, f32[128,256]{1,0:T(8,128)S(1)}, u32[]{:S(2)}, u32[]{:S(2)}) collective-permute-start(f32[128,256]{1,0:T(8,128)S(1)} %get-tuple-element.10), channel_id=1, source_target_pairs={{0,448},{1,449},{2,450},{3,451},{32,480},{33,481},{34,482},{35,483... | collective-permute-start | bytes 393224 | tf_op jit(solution)/shard_map/ppermute | solution.py:208
  3.7 0.7 %collective-permute-start.1 = (f32[128,256]{1,0:T(8,128)S(1)}, f32[128,256]{1,0:T(8,128)S(1)}, u32[]{:S(2)}, u32[]{:S(2)}) collective-permute-start(f32[128,256]{1,0:T(8,128)S(1)} %get-tuple-element.10), channel_id=1, source_target_pairs={{4,452},{5,453},{6,454},{7,455},{8,456},{9,457},{10,458},{11,459},... | collective-permute-start | bytes 393224 | tf_op jit(solution)/shard_map/ppermute | solution.py:208
  4.3 10.9 %collective-permute-start.4 = (f32[128,256]{1,0:T(8,128)S(1)}, f32[128,256]{1,0:T(8,128)S(1)}, u32[]{:S(2)}, u32[]{:S(2)}) collective-permute-start(f32[128,256]{1,0:T(8,128)S(1)} %get-tuple-element.12), channel_id=1, source_target_pairs={{0,28},{1,29},{2,30},{3,31},{4,8},{5,9},{6,10},{7,11},{8,4},{9,5},... | collective-permute-start | bytes 393224 | tf_op jit(solution)/shard_map/ppermute | solution.py:208
  15.3 0.0 collective-permute-done.refs_0_.y_got
  15.3 0.0 collective-permute-done.1.refs_1_.y_late
  15.3 0.0 copy-done
  15.4 0.0 copy-start.1
  15.4 0.0 copy-start.4
  15.4 0.0 copy-start.5
  15.4 0.0 copy-start.6
  15.4 6.0 %collective-permute-start.2 = (f32[2,128,256]{2,1,0:T(8,128)S(1)}, f32[2,128,256]{2,1,0:T(8,128)S(1)}, u32[]{:S(2)}, u32[]{:S(2)}) collective-permute-start(f32[2,128,256]{2,1,0:T(8,128)S(1)} %shard_map.82), channel_id=1, source_target_pairs={{0,64},{1,65},{2,66},{3,67},{4,68},{5,69},{6,70},{7,71},{8,72},{9,... | collective-permute-start | bytes 786440 | tf_op jit(solution)/shard_map/ppermute | solution.py:208
  21.4 1.9 %collective-permute-start.3 = (f32[128,256]{1,0:T(8,128)S(1)}, f32[128,256]{1,0:T(8,128)S(1)}, u32[]{:S(2)}, u32[]{:S(2)}) collective-permute-start(f32[128,256]{1,0:T(8,128)S(1)} %get-tuple-element.11), channel_id=1, source_target_pairs={{0,32},{1,33},{2,34},{3,35},{4,36},{5,37},{6,38},{7,39},{8,40},{9,... | collective-permute-start | bytes 393224 | tf_op jit(solution)/shard_map/ppermute | solution.py:208
  23.3 0.0 collective-permute-done.4.refs_0_.z_got
  23.3 1.9 %collective-permute-start.5 = (f32[2,128,256]{2,1,0:T(8,128)S(1)}, f32[2,128,256]{2,1,0:T(8,128)S(1)}, u32[]{:S(2)}, u32[]{:S(2)}) collective-permute-start(f32[2,128,256]{2,1,0:T(8,128)S(1)} %shard_map.83), channel_id=1, source_target_pairs={{0,4},{1,5},{2,6},{3,7},{4,0},{5,1},{6,2},{7,3},{8,12},{9,13},{10,... | collective-permute-start | bytes 786440 | tf_op jit(solution)/shard_map/ppermute | solution.py:208
  25.3 3.4 %collective-permute-start.7 = (f32[128,256]{1,0:T(8,128)S(1)}, f32[128,256]{1,0:T(8,128)S(1)}, u32[]{:S(2)}, u32[]{:S(2)}) collective-permute-start(f32[128,256]{1,0:T(8,128)S(1)} %get-tuple-element.14), channel_id=1, source_target_pairs={{0,1},{1,0},{2,3},{3,2},{32,33},{33,32},{34,35},{35,34},{64,65},{6... | collective-permute-start | bytes 393224 | tf_op jit(solution)/shard_map/ppermute | solution.py:208
  28.7 0.7 %collective-permute-start.8 = (f32[128,256]{1,0:T(8,128)S(1)}, f32[128,256]{1,0:T(8,128)S(1)}, u32[]{:S(2)}, u32[]{:S(2)}) collective-permute-start(f32[128,256]{1,0:T(8,128)S(1)} %get-tuple-element.14), channel_id=1, source_target_pairs={{4,5},{5,4},{6,7},{7,6},{8,9},{9,8},{10,11},{11,10},{12,13},{13,12... | collective-permute-start | bytes 393224 | tf_op jit(solution)/shard_map/ppermute | solution.py:208
  29.4 0.0 collective-permute-done.3.three
  29.4 4.0 %collective-permute-start.6 = (f32[128,256]{1,0:T(8,128)S(1)}, f32[128,256]{1,0:T(8,128)S(1)}, u32[]{:S(2)}, u32[]{:S(2)}) collective-permute-start(f32[128,256]{1,0:T(8,128)S(1)} %get-tuple-element.13), channel_id=1, source_target_pairs={{0,3},{1,2},{2,1},{3,0},{4,7},{5,6},{6,5},{7,4},{8,11},{9,10},{10,... | collective-permute-start | bytes 393224 | tf_op jit(solution)/shard_map/ppermute | solution.py:208
  34.0 0.0 copy-start.2
  34.0 0.0 copy-start.3
  34.1 0.0 collective-permute-done.2.y_pair
  34.1 0.0 copy-done.1
  34.1 0.0 copy-done.4
  34.1 0.0 copy-done.5
  34.1 0.0 copy-done.6
  34.1 2.2 %group_kernel.1.x_in = f32[256,128]{1,0:T(8,128)S(1)} custom-call(f32[256,128]{1,0:T(8,128)S(1)} %copy-done.4, bf16[2,256,128]{2,1,0:T(8,128)(2,1)S(1)} %copy-done.5, f32[2,128,128]{2,1,0:T(8,128)S(1)} %copy-done.6, bf16[1,1,9,256,256]{4,3,2,1,0:T(8,128)(2,1)S(1)} %copy-done.1, f32[1,1,9,128,256]{4,3,2,1,0:T(8,128)S(1)} %copy-done, ...), custom_call_target="tpu_custom_call" | custom-call | tf_op jit(solution)/shard_map/group_kernel/pallas_call | solution.py:248
  36.3 0.0 collective-permute-done.7.eight
  36.3 0.0 collective-permute-done.8.eight_late
  36.3 1.8 %collective-permute-done.6.seven = f32[128,256]{1,0:T(8,128)S(1)} collective-permute-done((f32[128,256]{1,0:T(8,128)S(1)}, f32[128,256]{1,0:T(8,128)S(1)}, u32[]{:S(2)}, u32[]{:S(2)}) %collective-permute-start.6) | collective-permute-done | bytes 131104 | tf_op jit(solution)/shard_map/ppermute | solution.py:208
  38.1 0.0 collective-permute-done.5.z_pair
  38.1 0.0 copy-done.2
  38.1 0.0 copy-done.3
  38.1 2.8 %leaf_kernel.1 = bf16[512,128]{1,0:T(8,128)(2,1)} custom-call(f32[256,128]{1,0:T(8,128)S(1)} %group_kernel.1.x_in, bf16[1,1,9,256,256]{4,3,2,1,0:T(8,128)(2,1)S(1)} %copy-done.1, f32[1,1,9,128,256]{4,3,2,1,0:T(8,128)S(1)} %copy-done, f32[128,256]{1,0:T(8,128)S(1)} %collective-permute-done.4.refs_0_.z_got, f32[2,128,256]{2,1,0:T(8,128)S(1)} %collective-permute-done.5.z_pair, ...), custom_call_target="tpu_custom_call" | custom-call | tf_op jit(solution)/shard_map/leaf_kernel/pallas_call | solution.py:260
  (2 shorter events, 0.0 us)
Async XLA Ops:
  0.0 15.3 %copy-start = (f32[1,1,9,128,256]{4,3,2,1,0:T(8,128)S(1)}, f32[1,1,9,128,256]{4,3,2,1,0:T(8,128)}, u32[]{:S(2)}) copy-start(f32[1,1,9,128,256]{4,3,2,1,0:T(8,128)} %own.7) | copy-start | bytes 3538948
  1.3 14.0 %collective-permute-start = (f32[128,256]{1,0:T(8,128)S(1)}, f32[128,256]{1,0:T(8,128)S(1)}, u32[]{:S(2)}, u32[]{:S(2)}) collective-permute-start(f32[128,256]{1,0:T(8,128)S(1)} %get-tuple-element.10), channel_id=1, source_target_pairs={{0,448},{1,449},{2,450},{3,451},{32,480},{33,481},{34,482},{35,483... | collective-permute-start | bytes 393224 | tf_op jit(solution)/shard_map/ppermute | solution.py:208
  3.7 11.6 %collective-permute-start.1 = (f32[128,256]{1,0:T(8,128)S(1)}, f32[128,256]{1,0:T(8,128)S(1)}, u32[]{:S(2)}, u32[]{:S(2)}) collective-permute-start(f32[128,256]{1,0:T(8,128)S(1)} %get-tuple-element.10), channel_id=1, source_target_pairs={{4,452},{5,453},{6,454},{7,455},{8,456},{9,457},{10,458},{11,459},... | collective-permute-start | bytes 393224 | tf_op jit(solution)/shard_map/ppermute | solution.py:208
  4.3 19.0 %collective-permute-start.4 = (f32[128,256]{1,0:T(8,128)S(1)}, f32[128,256]{1,0:T(8,128)S(1)}, u32[]{:S(2)}, u32[]{:S(2)}) collective-permute-start(f32[128,256]{1,0:T(8,128)S(1)} %get-tuple-element.12), channel_id=1, source_target_pairs={{0,28},{1,29},{2,30},{3,31},{4,8},{5,9},{6,10},{7,11},{8,4},{9,5},... | collective-permute-start | bytes 393224 | tf_op jit(solution)/shard_map/ppermute | solution.py:208
  15.4 18.7 %copy-start.1 = (bf16[1,1,9,256,256]{4,3,2,1,0:T(8,128)(2,1)S(1)}, bf16[1,1,9,256,256]{4,3,2,1,0:T(8,128)(2,1)}, u32[]{:S(2)}) copy-start(bf16[1,1,9,256,256]{4,3,2,1,0:T(8,128)(2,1)} %node_y.3) | copy-start | bytes 3538948
  15.4 18.7 %copy-start.4 = (f32[256,128]{1,0:T(8,128)S(1)}, f32[256,128]{1,0:T(8,128)}, u32[]{:S(2)}) copy-start(f32[256,128]{1,0:T(8,128)} %left.1) | copy-start | bytes 393220
  15.4 18.7 %copy-start.5 = (bf16[2,256,128]{2,1,0:T(8,128)(2,1)S(1)}, bf16[2,256,128]{2,1,0:T(8,128)(2,1)}, u32[]{:S(2)}) copy-start(bf16[2,256,128]{2,1,0:T(8,128)(2,1)} %vectors.1) | copy-start | bytes 393220
  15.4 18.7 %copy-start.6 = (f32[2,128,128]{2,1,0:T(8,128)S(1)}, f32[2,128,128]{2,1,0:T(8,128)}, u32[]{:S(2)}) copy-start(f32[2,128,128]{2,1,0:T(8,128)} %factors.1) | copy-start | bytes 393220
  15.4 18.6 %collective-permute-start.2 = (f32[2,128,256]{2,1,0:T(8,128)S(1)}, f32[2,128,256]{2,1,0:T(8,128)S(1)}, u32[]{:S(2)}, u32[]{:S(2)}) collective-permute-start(f32[2,128,256]{2,1,0:T(8,128)S(1)} %shard_map.82), channel_id=1, source_target_pairs={{0,64},{1,65},{2,66},{3,67},{4,68},{5,69},{6,70},{7,71},{8,72},{9,... | collective-permute-start | bytes 786440 | tf_op jit(solution)/shard_map/ppermute | solution.py:208
  21.4 8.0 %collective-permute-start.3 = (f32[128,256]{1,0:T(8,128)S(1)}, f32[128,256]{1,0:T(8,128)S(1)}, u32[]{:S(2)}, u32[]{:S(2)}) collective-permute-start(f32[128,256]{1,0:T(8,128)S(1)} %get-tuple-element.11), channel_id=1, source_target_pairs={{0,32},{1,33},{2,34},{3,35},{4,36},{5,37},{6,38},{7,39},{8,40},{9,... | collective-permute-start | bytes 393224 | tf_op jit(solution)/shard_map/ppermute | solution.py:208
  23.3 14.8 %collective-permute-start.5 = (f32[2,128,256]{2,1,0:T(8,128)S(1)}, f32[2,128,256]{2,1,0:T(8,128)S(1)}, u32[]{:S(2)}, u32[]{:S(2)}) collective-permute-start(f32[2,128,256]{2,1,0:T(8,128)S(1)} %shard_map.83), channel_id=1, source_target_pairs={{0,4},{1,5},{2,6},{3,7},{4,0},{5,1},{6,2},{7,3},{8,12},{9,13},{10,... | collective-permute-start | bytes 786440 | tf_op jit(solution)/shard_map/ppermute | solution.py:208
  25.3 11.1 %collective-permute-start.7 = (f32[128,256]{1,0:T(8,128)S(1)}, f32[128,256]{1,0:T(8,128)S(1)}, u32[]{:S(2)}, u32[]{:S(2)}) collective-permute-start(f32[128,256]{1,0:T(8,128)S(1)} %get-tuple-element.14), channel_id=1, source_target_pairs={{0,1},{1,0},{2,3},{3,2},{32,33},{33,32},{34,35},{35,34},{64,65},{6... | collective-permute-start | bytes 393224 | tf_op jit(solution)/shard_map/ppermute | solution.py:208
  28.7 7.7 %collective-permute-start.8 = (f32[128,256]{1,0:T(8,128)S(1)}, f32[128,256]{1,0:T(8,128)S(1)}, u32[]{:S(2)}, u32[]{:S(2)}) collective-permute-start(f32[128,256]{1,0:T(8,128)S(1)} %get-tuple-element.14), channel_id=1, source_target_pairs={{4,5},{5,4},{6,7},{7,6},{8,9},{9,8},{10,11},{11,10},{12,13},{13,12... | collective-permute-start | bytes 393224 | tf_op jit(solution)/shard_map/ppermute | solution.py:208
  29.4 8.7 %collective-permute-start.6 = (f32[128,256]{1,0:T(8,128)S(1)}, f32[128,256]{1,0:T(8,128)S(1)}, u32[]{:S(2)}, u32[]{:S(2)}) collective-permute-start(f32[128,256]{1,0:T(8,128)S(1)} %get-tuple-element.13), channel_id=1, source_target_pairs={{0,3},{1,2},{2,1},{3,0},{4,7},{5,6},{6,5},{7,4},{8,11},{9,10},{10,... | collective-permute-start | bytes 393224 | tf_op jit(solution)/shard_map/ppermute | solution.py:208
  34.0 4.1 %copy-start.2 = (bf16[512,256]{1,0:T(8,128)(2,1)S(1)}, bf16[512,256]{1,0:T(8,128)(2,1)}, u32[]{:S(2)}) copy-start(bf16[512,256]{1,0:T(8,128)(2,1)} %leaf_v.1) | copy-start | bytes 786436
  34.0 4.1 %copy-start.3 = (f32[1,1,256,256]{3,2,1,0:T(8,128)S(1)}, f32[1,1,256,256]{3,2,1,0:T(8,128)}, u32[]{:S(2)}) copy-start(f32[1,1,256,256]{3,2,1,0:T(8,128)} %leaf_t.1) | copy-start | bytes 786436
where the time goes:
time: 41.2 us; the launch traced here: 40.9 us
  starting transfers between devices  31.8 us (77%)
  Pallas kernels  6.35 us (15%)
  waiting for transfers between devices  1.77 us (4%)
  between operations  0.9 us (2%)
    ppermute x9, starting transfers between devices, exchange(): return lax.ppermute(block, ('group', 'leaf'), pairs)  31.8 us
    pallas_call x1, Pallas kernels, body(): pl.pallas_call(leaf_kernel, out_shape=jax.ShapeDtypeStruct((512, 128), bf...  2.8 us
    pallas_call x1, Pallas kernels, body(): pl.pallas_call(group_kernel, out_shape=pltpu.VMEM((256, 128), f32), in_sp...  2.21 us
    ppermute x9, waiting for transfers between devices, exchange(): return lax.ppermute(block, ('group', 'leaf'), pairs)  1.77 us
    pallas_call x1, Pallas kernels, pieces(): pl.pallas_call(pieces_kernel, out_shape=(shape,) * 5, in_specs=[ANY], out...  1.29 us
  transfers between devices with their start and end apart: 9, of which 1 were waited for; matrix products, arithmetic and copies ran while one was open for 0% of the time, Pallas kernels for 6%

commit v1 on v0

--- a/solution.py
+++ b/solution.py
@@ -8,7 +8,6 @@
 
 ANY = pl.BlockSpec(memory_space=pl.ANY)
 VMEM = pl.BlockSpec(memory_space=pltpu.VMEM)
-SMEM = pl.BlockSpec(memory_space=pltpu.SMEM)
 SMALL = pltpu.CompilerParams(vmem_limit_bytes=8 << 20)
 f32 = jnp.float32
 bf16 = jnp.bfloat16
@@ -51,12 +50,12 @@
     return group >> 1, group & 1, leaf >> 2, leaf & 3
 
 
-def is_ahead(z):
+def y_ahead(y, z):
+    return (z == 0) | (z == 3)
+
+
+def eight_ahead(y, z):
     return z == 0
-
-
-def ahead():
-    return is_ahead(lax.axis_index("leaf") >> 2)
 
 
 def pieces_kernel(node_t, y_send, z_send, seven, eight, three, sems):
@@ -99,7 +98,8 @@
         if len(refs) == 2:
             out[1] = refs[0][...]
         else:
-            out[1] = jnp.where(ahead(), refs[0][...], refs[1][...])
+            y, _, z, _ = places()
+            out[1] = jnp.where(y_ahead(y, z), refs[0][...], refs[1][...])
 
     return pl.pallas_call(
         kernel,
@@ -107,7 +107,7 @@
         in_specs=[VMEM] * (1 + len(received)),
         out_specs=VMEM,
         compiler_params=SMALL,
-    )(own, *[in_vmem(array) for array in received])
+    )(*[in_vmem(array) for array in (own, *received)])
 
 
 def place_rows(high_ref, low_ref, slot, bit, value):
@@ -129,15 +129,16 @@
         x_ref[...] = x_ref[...] - weighted
 
 
-def group_kernel(
-    left, vectors, factors, node_y, own, y_got, y_late, y_pair, three, x_out,
-    high_ref, low_ref,
-):
-    y, core, _, _ = places()
+def root_kernel(left, vectors, factors, own, y_got, y_late, three, x_out, high_ref, low_ref):
+    y, core, z, _ = places()
     outer = ring_outer(y)
-    row = jnp.where(outer, 0, 1)
-    bits = [(y >> 2) & 1, (y >> 1) & 1, y & 1, core]
-
+    bits = [(y >> 2) & 1, (y >> 1) & 1]
+    ring_bit = jnp.where(outer, bits[0], bits[1])
+    ring_own = jnp.where(outer, own[0, 0, 0], own[0, 0, 1])
+    place_rows(high_ref, low_ref, 0, ring_bit, ring_own)
+    place_rows(high_ref, low_ref, 0, 1 - ring_bit, jnp.where(y_ahead(y, z), y_got[...], y_late[...]))
+    place_rows(high_ref, low_ref, 1, core, own[0, 0, 3])
+    place_rows(high_ref, low_ref, 1, 1 - core, three[...])
     x = left[...]
     for panel in (1, 0):
         vector = vectors[panel]
@@ -153,41 +154,64 @@
         x = x - exact_times(vector, scaled)
     x_out[...] = x
 
+
+def group_kernel(x_in, high_in, low_in, node_y, own, y_pair, x_out, high_ref, low_ref):
+    y, core, _, _ = places()
+    outer = ring_outer(y)
+    bits = [(y >> 2) & 1, (y >> 1) & 1, y & 1, core]
+    pair_bit = jnp.where(outer, bits[1], bits[0])
+    pair_own = jnp.where(outer, own[0, 0, 1], own[0, 0, 0])
+    place_rows(high_ref, low_ref, 0, pair_bit, pair_own)
+    place_rows(high_ref, low_ref, 0, 1 - pair_bit, y_pair[1])
+    place_rows(high_ref, low_ref, 1, bits[2], own[0, 0, 2])
+    place_rows(high_ref, low_ref, 1, 1 - bits[2], y_pair[0])
+    x_out[...] = x_in[...]
+    terms = [
+        (jnp.where(outer, high_in[0], high_ref[0]), jnp.where(outer, low_in[0], low_ref[0])),
+        (jnp.where(outer, high_ref[0], high_in[0]), jnp.where(outer, low_ref[0], low_in[0])),
+        (high_ref[1], low_ref[1]),
+        (high_in[1], low_in[1]),
+    ]
+    for i, (high, low) in enumerate(terms):
+        tree_step(x_out, high, low, node_y.at[0, 0, i], bits[i])
+
+
+def middle_kernel(x_in, node_y, own, z_got, z_pair, eight, eight_late, x_out, high_out, low_out, high_ref, low_ref):
+    y, _, z, x_place = places()
+    outer = ring_outer(z)
+    row = jnp.where(outer, 0, 1)
+    bits = [(z >> 2) & 1, (z >> 1) & 1, z & 1]
     ring_bit = jnp.where(outer, bits[0], bits[1])
     pair_bit = jnp.where(outer, bits[1], bits[0])
-    for i in range(4):
-        place_rows(high_ref, low_ref, i, bits[i], own[0, 0, i])
-    place_rows(high_ref, low_ref, row, 1 - ring_bit, jnp.where(ahead(), y_got[...], y_late[...]))
-    place_rows(high_ref, low_ref, 1 - row, 1 - pair_bit, y_pair[1])
-    place_rows(high_ref, low_ref, 2, 1 - bits[2], y_pair[0])
-    place_rows(high_ref, low_ref, 3, 1 - bits[3], three[...])
-    for i in range(4):
-        tree_step(x_out, high_ref[i], low_ref[i], node_y.at[0, 0, i], bits[i])
-
-
-def leaf_kernel(
-    x_in, node_y, own, z_got, z_pair, seven, eight, eight_late, leaf_v, leaf_t, leaf_map, out,
-    x_ref, high_ref, low_ref,
-):
-    _, _, z, x_place = places()
-    outer = ring_outer(z)
-    row = jnp.where(outer, 0, 1)
-    bits = [(z >> 2) & 1, (z >> 1) & 1, z & 1, (x_place >> 1) & 1, x_place & 1]
-    x_ref[...] = x_in[...]
-    flipped = leaf_map[0, 0] != lax.axis_index("leaf")
-    last = jnp.where(flipped, 1 - bits[4], bits[4])
-    lows = bits[:4] + [last]
-    ring_bit = jnp.where(outer, bits[0], bits[1])
-    pair_bit = jnp.where(outer, bits[1], bits[0])
-    for i in range(5):
+    x_out[...] = x_in[...]
+    for i in range(3):
         place_rows(high_ref, low_ref, i, bits[i], own[0, 0, 4 + i])
     place_rows(high_ref, low_ref, row, 1 - ring_bit, z_got[...])
     place_rows(high_ref, low_ref, 1 - row, 1 - pair_bit, z_pair[1])
     place_rows(high_ref, low_ref, 2, 1 - bits[2], z_pair[0])
-    place_rows(high_ref, low_ref, 3, 1 - bits[3], seven[...])
-    place_rows(high_ref, low_ref, 4, 1 - bits[4], jnp.where(ahead(), eight[...], eight_late[...]))
-    for i in range(5):
-        tree_step(x_ref, high_ref[i], low_ref[i], node_y.at[0, 0, 4 + i], lows[i])
+    last = x_place & 1
+    place_rows(high_out, low_out, 0, last, own[0, 0, 8])
+    place_rows(high_out, low_out, 0, 1 - last, jnp.where(eight_ahead(y, z), eight[...], eight_late[...]))
+    for i in range(3):
+        tree_step(x_out, high_ref[i], low_ref[i], node_y.at[0, 0, 4 + i], bits[i])
+
+
+def leaf_kernel(
+    x_in, high_in, low_in, node_y, own, seven, leaf_v, leaf_t, leaf_map, out,
+    x_ref, high_ref, low_ref, map_ref, sem,
+):
+    _, _, _, x_place = places()
+    load = pltpu.make_async_copy(leaf_map, map_ref, sem)
+    load.start()
+    bit = (x_place >> 1) & 1
+    last = x_place & 1
+    x_ref[...] = x_in[...]
+    place_rows(high_ref, low_ref, 0, bit, own[0, 0, 7])
+    place_rows(high_ref, low_ref, 0, 1 - bit, seven[...])
+    tree_step(x_ref, high_ref[0], low_ref[0], node_y.at[0, 0, 7], bit)
+    load.wait()
+    flipped = map_ref[0, 0] != lax.axis_index("leaf")
+    tree_step(x_ref, high_in[0], low_in[0], node_y.at[0, 0, 8], jnp.where(flipped, 1 - last, last))
     x = x_ref[...]
     projected = lax.dot_general(
         leaf_v[:256], x.astype(bf16), (((0,), (0,)), ((), ())), preferred_element_type=f32
@@ -197,21 +221,28 @@
     out[256:] = (-mul(leaf_v[256:], solved)).astype(bf16)
 
 
-def exchange(block, partner, planes=None):
+def call(kernel, arrays, outs, scratch=()):
+    return pl.pallas_call(
+        kernel,
+        out_shape=tuple(pltpu.VMEM(shape, dtype) for shape, dtype in outs),
+        in_specs=[VMEM] * len(arrays),
+        out_specs=(VMEM,) * len(outs),
+        scratch_shapes=list(scratch),
+        compiler_params=SMALL,
+    )(*[in_vmem(array) for array in arrays])
+
+
+def exchange(block, partner, chosen=lambda y, z: True):
     pairs = []
     for g in range(16):
         for j in range(32):
             place = (g >> 1, g & 1, j >> 2, j & 3)
-            if planes is None or planes(place[2]):
+            if chosen(place[0], place[2]):
                 y, core, z, x = partner(*place)
                 pairs.append((g * 32 + j, (y * 2 + core) * 32 + z * 4 + x))
     return lax.ppermute(block, ("group", "leaf"), pairs)
 
 
-def is_behind(z):
-    return not is_ahead(z)
-
-
 def body(left_vectors, panel_vectors, panel_factors, node_y, node_t, leaf_v, leaf_t, leaf_map):
     def y_ring(y, core, z, x):
         return ring_partner(y), core, z, x
@@ -235,40 +266,40 @@
         return y, 1 - core, z, x
 
     y_send, z_send, seven, eight, three = pieces(pltpu.with_memory_space_constraint(node_t, pltpu.HBM))
-    own, node_y, leaf_v, leaf_t = [in_vmem(array) for array in (node_t, node_y, leaf_v, leaf_t)]
-    y_got = [exchange(y_send, y_ring, is_ahead)]
-    eight_got = [exchange(eight, x_next, is_ahead)]
+    own = node_t
+    y_got = [exchange(y_send, y_ring, y_ahead)]
+    eight_got = [exchange(eight, x_next, eight_ahead)]
     z_got = exchange(z_send, z_ring)
-    y_got.append(exchange(y_send, y_ring, is_behind))
-    eight_got.append(exchange(eight, x_next, is_behind))
+    y_got.append(exchange(y_send, y_ring, lambda y, z: not y_ahead(y, z)))
+    eight_got.append(exchange(eight, x_next, lambda y, z: not eight_ahead(y, z)))
     three_got = exchange(three, other_core)
     y_pair = exchange(join(own, y_got, 2), y_next)
     z_pair = exchange(join(own, [z_got], 6), z_next)
     seven_got = exchange(seven, x_far)
-    x = pl.pallas_call(
-        group_kernel,
-        out_shape=pltpu.VMEM((256, 128), f32),
-        in_specs=[VMEM] * 9,
-        out_specs=VMEM,
-        scratch_shapes=[pltpu.VMEM((4, 256, 256), bf16)] * 2,
-        name="group_kernel",
-        compiler_params=SMALL,
-    )(
-        in_vmem(left_vectors), in_vmem(panel_vectors), in_vmem(panel_factors), node_y, own,
-        *[in_vmem(array) for array in (*y_got, y_pair, three_got)],
+    term = pltpu.VMEM((2, 256, 256), bf16)
+    root, high, low = call(
+        root_kernel,
+        [left_vectors, panel_vectors, panel_factors, own, *y_got, three_got],
+        [((256, 128), f32), ((2, 256, 256), bf16), ((2, 256, 256), bf16)],
     )
+    (x,) = call(group_kernel, [root, high, low, node_y, own, y_pair], [((256, 128), f32)], (term, term))
+    term = pltpu.VMEM((3, 256, 256), bf16)
+    x, high, low = call(
+        middle_kernel,
+        [x, node_y, own, z_got, z_pair, *eight_got],
+        [((256, 128), f32), ((1, 256, 256), bf16), ((1, 256, 256), bf16)],
+        (term, term),
+    )
+    term = pltpu.VMEM((1, 256, 256), bf16)
     return pl.pallas_call(
         leaf_kernel,
         out_shape=jax.ShapeDtypeStruct((512, 128), bf16),
-        in_specs=[VMEM] * 10 + [SMEM],
+        in_specs=[VMEM] * 8 + [ANY],
         out_specs=VMEM,
-        scratch_shapes=[pltpu.VMEM((256, 128), f32)] + [pltpu.VMEM((5, 256, 256), bf16)] * 2,
+        scratch_shapes=[pltpu.VMEM((256, 128), f32), term, term, pltpu.SMEM((1, 1), jnp.int32), pltpu.SemaphoreType.DMA],
         name="leaf_kernel",
         compiler_params=SMALL,
-    )(
-        in_vmem(x), node_y, own, *[in_vmem(array) for array in (z_got, z_pair, seven_got, *eight_got)],
-        leaf_v, leaf_t, leaf_map,
-    )
+    )(*[in_vmem(array) for array in (x, high, low, node_y, own, seven_got, leaf_v, leaf_t)], leaf_map)
 
 
 def solution(mesh):

time: 41.2 us -> 40.9 us (level)
  waiting for transfers between devices: 1.77 us -> 0.8 us
  Pallas kernels: 6.35 us -> 6.82 us
    ppermute x9, waiting for transfers between devices: 1.77 us -> 0.8 us  [exchange(): return lax.ppermute(block, ('group', 'leaf'), pairs)]
    pallas_call x1 -> x3, Pallas kernels: 2.21 us -> 3.15 us  [call(): pl.pallas_call(kernel, out_shape=tuple((pltpu.VMEM(shape, dtype) for shap...]
    pallas_call x1, Pallas kernels: 2.8 us -> 2.33 us  [body(): pl.pallas_call(leaf_kernel, out_shape=jax.ShapeDtypeStruct((512, 128), bf...]
  transfers between devices with their start and end apart: 9 -> 9, of which waited for: 1 -> 1; matrix products, arithmetic and copies ran while one was open for 0% -> 0% of each run, Pallas kernels for 6% -> 8%
where the time goes in v1:
time: 40.9 us; the launch traced here: 40.6 us
  starting transfers between devices  32 us (78%)
  Pallas kernels  6.82 us (17%)
  between operations  0.92 us (2%)
  waiting for transfers between devices  0.8 us (2%)
    ppermute x9, starting transfers between devices, exchange(): return lax.ppermute(block, ('group', 'leaf'), pairs)  32 us
    pallas_call x3, Pallas kernels, call(): pl.pallas_call(kernel, out_shape=tuple((pltpu.VMEM(shape, dtype) for shap...  3.15 us
    pallas_call x1, Pallas kernels, body(): pl.pallas_call(leaf_kernel, out_shape=jax.ShapeDtypeStruct((512, 128), bf...  2.33 us
    pallas_call x1, Pallas kernels, pieces(): pl.pallas_call(pieces_kernel, out_shape=(shape,) * 5, in_specs=[ANY], out...  1.29 us
  transfers between devices with their start and end apart: 9, of which 1 were waited for; matrix products, arithmetic and copies ran while one was open for 0% of the time, Pallas kernels for 8%

profile of v1, /device:TPU:16, one launch (start us, length us, event | category | flops | bytes accessed | tf_op | source)
XLA Modules:
  0.0 40.6 jit_solution(5694553002598189561)
XLA Ops:
  0.0 0.0 copy-start
  0.0 1.3 %pieces.1 = (f32[128,256]{1,0:T(8,128)S(1)}, f32[128,256]{1,0:T(8,128)S(1)}, f32[128,256]{1,0:T(8,128)S(1)}, f32[128,256]{1,0:T(8,128)S(1)}, f32[128,256]{1,0:T(8,128)S(1)}) custom-call(f32[1,1,9,128,256]{4,3,2,1,0:T(8,128)} %own.11), custom_call_target="tpu_custom_call" | custom-call | tf_op jit(solution)/shard_map/pieces/pallas_call | solution.py:83
  1.3 2.4 %collective-permute-start = (f32[128,256]{1,0:T(8,128)S(1)}, f32[128,256]{1,0:T(8,128)S(1)}, u32[]{:S(2)}, u32[]{:S(2)}) collective-permute-start(f32[128,256]{1,0:T(8,128)S(1)} %get-tuple-element.16), channel_id=1, source_target_pairs={{0,448},{1,449},{2,450},{3,451},{12,460},{13,461},{14,462},{15,463... | collective-permute-start | bytes 393224 | tf_op jit(solution)/shard_map/ppermute | solution.py:243
  3.7 0.7 %collective-permute-start.1 = (f32[128,256]{1,0:T(8,128)S(1)}, f32[128,256]{1,0:T(8,128)S(1)}, u32[]{:S(2)}, u32[]{:S(2)}) collective-permute-start(f32[128,256]{1,0:T(8,128)S(1)} %get-tuple-element.16), channel_id=1, source_target_pairs={{4,452},{5,453},{6,454},{7,455},{8,456},{9,457},{10,458},{11,459},... | collective-permute-start | bytes 393224 | tf_op jit(solution)/shard_map/ppermute | solution.py:243
  4.3 10.9 %collective-permute-start.4 = (f32[128,256]{1,0:T(8,128)S(1)}, f32[128,256]{1,0:T(8,128)S(1)}, u32[]{:S(2)}, u32[]{:S(2)}) collective-permute-start(f32[128,256]{1,0:T(8,128)S(1)} %get-tuple-element.21), channel_id=1, source_target_pairs={{0,28},{1,29},{2,30},{3,31},{4,8},{5,9},{6,10},{7,11},{8,4},{9,5},... | collective-permute-start | bytes 393224 | tf_op jit(solution)/shard_map/ppermute | solution.py:243
  15.3 0.0 collective-permute-done.y_got.refs_0_
  15.3 0.0 collective-permute-done.1.y_late.refs_1_
  15.3 0.0 copy-done
  15.4 0.0 copy-start.4
  15.4 0.0 copy-start.5
  15.4 0.0 copy-start.6
  15.4 6.0 %collective-permute-start.3 = (f32[2,128,256]{2,1,0:T(8,128)S(1)}, f32[2,128,256]{2,1,0:T(8,128)S(1)}, u32[]{:S(2)}, u32[]{:S(2)}) collective-permute-start(f32[2,128,256]{2,1,0:T(8,128)S(1)} %shard_map.83), channel_id=1, source_target_pairs={{0,64},{1,65},{2,66},{3,67},{4,68},{5,69},{6,70},{7,71},{8,72},{9,... | collective-permute-start | bytes 786440 | tf_op jit(solution)/shard_map/ppermute | solution.py:243
  21.4 1.9 %collective-permute-start.2 = (f32[128,256]{1,0:T(8,128)S(1)}, f32[128,256]{1,0:T(8,128)S(1)}, u32[]{:S(2)}, u32[]{:S(2)}) collective-permute-start(f32[128,256]{1,0:T(8,128)S(1)} %get-tuple-element.17), channel_id=1, source_target_pairs={{0,32},{1,33},{2,34},{3,35},{4,36},{5,37},{6,38},{7,39},{8,40},{9,... | collective-permute-start | bytes 393224 | tf_op jit(solution)/shard_map/ppermute | solution.py:243
  23.3 0.0 collective-permute-done.4.refs_0_.z_got
  23.3 0.0 copy-start.1
  23.3 2.1 %collective-permute-start.5 = (f32[2,128,256]{2,1,0:T(8,128)S(1)}, f32[2,128,256]{2,1,0:T(8,128)S(1)}, u32[]{:S(2)}, u32[]{:S(2)}) collective-permute-start(f32[2,128,256]{2,1,0:T(8,128)S(1)} %shard_map.85), channel_id=1, source_target_pairs={{0,4},{1,5},{2,6},{3,7},{4,0},{5,1},{6,2},{7,3},{8,12},{9,13},{10,... | collective-permute-start | bytes 786440 | tf_op jit(solution)/shard_map/ppermute | solution.py:243
  25.4 3.4 %collective-permute-start.6 = (f32[128,256]{1,0:T(8,128)S(1)}, f32[128,256]{1,0:T(8,128)S(1)}, u32[]{:S(2)}, u32[]{:S(2)}) collective-permute-start(f32[128,256]{1,0:T(8,128)S(1)} %get-tuple-element.22), channel_id=1, source_target_pairs={{0,1},{1,0},{2,3},{3,2},{32,33},{33,32},{34,35},{35,34},{64,65},{6... | collective-permute-start | bytes 393224 | tf_op jit(solution)/shard_map/ppermute | solution.py:243
  28.8 0.7 %collective-permute-start.7 = (f32[128,256]{1,0:T(8,128)S(1)}, f32[128,256]{1,0:T(8,128)S(1)}, u32[]{:S(2)}, u32[]{:S(2)}) collective-permute-start(f32[128,256]{1,0:T(8,128)S(1)} %get-tuple-element.22), channel_id=1, source_target_pairs={{4,5},{5,4},{6,7},{7,6},{8,9},{9,8},{10,11},{11,10},{12,13},{13,12... | collective-permute-start | bytes 393224 | tf_op jit(solution)/shard_map/ppermute | solution.py:243
  29.5 0.0 collective-permute-done.2.three
  29.5 4.0 %collective-permute-start.8 = (f32[128,256]{1,0:T(8,128)S(1)}, f32[128,256]{1,0:T(8,128)S(1)}, u32[]{:S(2)}, u32[]{:S(2)}) collective-permute-start(f32[128,256]{1,0:T(8,128)S(1)} %get-tuple-element.26), channel_id=1, source_target_pairs={{0,3},{1,2},{2,1},{3,0},{4,7},{5,6},{6,5},{7,4},{8,11},{9,10},{10,... | collective-permute-start | bytes 393224 | tf_op jit(solution)/shard_map/ppermute | solution.py:243
  34.2 0.0 copy-done.4
  34.2 0.0 copy-done.5
  34.2 0.0 copy-done.6
  34.2 1.1 %shard_map.82 = (f32[256,128]{1,0:T(8,128)S(1)}, bf16[2,256,256]{2,1,0:T(8,128)(2,1)S(1)}, bf16[2,256,256]{2,1,0:T(8,128)(2,1)S(1)}) custom-call(f32[256,128]{1,0:T(8,128)S(1)} %copy-done.4, bf16[2,256,128]{2,1,0:T(8,128)(2,1)S(1)} %copy-done.5, f32[2,128,128]{2,1,0:T(8,128)S(1)} %copy-done.6, f32[1,1,9,128,256]{4,3,2,1,0:T(8,128)S(1)} %copy-done, ...), custom_call_target="tpu_custom_call" | custom-call | tf_op jit(solution)/shard_map/pallas_call | solution.py:225
  35.3 0.0 collective-permute-done.3.y_pair
  35.3 0.0 copy-done.1
  35.3 1.2 %shard_map.84.x_in = f32[256,128]{1,0:T(8,128)S(1)} custom-call(f32[256,128]{1,0:T(8,128)S(1)} %get-tuple-element.18.x_in, bf16[2,256,256]{2,1,0:T(8,128)(2,1)S(1)} %get-tuple-element.19.high_in, bf16[2,256,256]{2,1,0:T(8,128)(2,1)S(1)} %get-tuple-element.20.low_in, bf16[1,1,9,256,256]{4,3,2,1,0:T(8,128)(2,1)S(1)} %copy-done.1, ...), custom_call_target="tpu_custom_call" | custom-call | tf_op jit(solution)/shard_map/pallas_call | solution.py:225
  36.6 0.0 copy-start.2
  36.6 0.0 copy-start.3
  36.6 0.0 collective-permute-done.6.eight
  36.6 0.0 collective-permute-done.7.eight_late
  36.6 0.0 collective-permute-done.5.z_pair
  36.6 0.8 %shard_map.86 = (f32[256,128]{1,0:T(8,128)S(1)}, bf16[1,256,256]{2,1,0:T(8,128)(2,1)S(1)}, bf16[1,256,256]{2,1,0:T(8,128)(2,1)S(1)}) custom-call(f32[256,128]{1,0:T(8,128)S(1)} %shard_map.84.x_in, bf16[1,1,9,256,256]{4,3,2,1,0:T(8,128)(2,1)S(1)} %copy-done.1, f32[1,1,9,128,256]{4,3,2,1,0:T(8,128)S(1)} %copy-done, ...), custom_call_target="tpu_custom_call" | custom-call | tf_op jit(solution)/shard_map/pallas_call | solution.py:225
  37.4 0.8 %collective-permute-done.8.seven = f32[128,256]{1,0:T(8,128)S(1)} collective-permute-done((f32[128,256]{1,0:T(8,128)S(1)}, f32[128,256]{1,0:T(8,128)S(1)}, u32[]{:S(2)}, u32[]{:S(2)}) %collective-permute-start.8) | collective-permute-done | bytes 131104 | tf_op jit(solution)/shard_map/ppermute | solution.py:243
  38.2 0.0 copy-done.2
  38.2 0.0 copy-done.3
  38.2 2.3 %leaf_kernel.1 = bf16[512,128]{1,0:T(8,128)(2,1)} custom-call(f32[256,128]{1,0:T(8,128)S(1)} %get-tuple-element.23.x_in, bf16[1,256,256]{2,1,0:T(8,128)(2,1)S(1)} %get-tuple-element.24.high_in, bf16[1,256,256]{2,1,0:T(8,128)(2,1)S(1)} %get-tuple-element.25.low_in, bf16[1,1,9,256,256]{4,3,2,1,0:T(8,128)(2,1)S(1)} %copy-done.1, ...), custom_call_target="tpu_custom_call" | custom-call | tf_op jit(solution)/shard_map/leaf_kernel/pallas_call | solution.py:294
  (2 shorter events, 0.0 us)
Async XLA Ops:
  0.0 15.3 %copy-start = (f32[1,1,9,128,256]{4,3,2,1,0:T(8,128)S(1)}, f32[1,1,9,128,256]{4,3,2,1,0:T(8,128)}, u32[]{:S(2)}) copy-start(f32[1,1,9,128,256]{4,3,2,1,0:T(8,128)} %own.11) | copy-start | bytes 3538948
  1.3 14.0 %collective-permute-start = (f32[128,256]{1,0:T(8,128)S(1)}, f32[128,256]{1,0:T(8,128)S(1)}, u32[]{:S(2)}, u32[]{:S(2)}) collective-permute-start(f32[128,256]{1,0:T(8,128)S(1)} %get-tuple-element.16), channel_id=1, source_target_pairs={{0,448},{1,449},{2,450},{3,451},{12,460},{13,461},{14,462},{15,463... | collective-permute-start | bytes 393224 | tf_op jit(solution)/shard_map/ppermute | solution.py:243
  3.7 11.6 %collective-permute-start.1 = (f32[128,256]{1,0:T(8,128)S(1)}, f32[128,256]{1,0:T(8,128)S(1)}, u32[]{:S(2)}, u32[]{:S(2)}) collective-permute-start(f32[128,256]{1,0:T(8,128)S(1)} %get-tuple-element.16), channel_id=1, source_target_pairs={{4,452},{5,453},{6,454},{7,455},{8,456},{9,457},{10,458},{11,459},... | collective-permute-start | bytes 393224 | tf_op jit(solution)/shard_map/ppermute | solution.py:243
  4.3 18.9 %collective-permute-start.4 = (f32[128,256]{1,0:T(8,128)S(1)}, f32[128,256]{1,0:T(8,128)S(1)}, u32[]{:S(2)}, u32[]{:S(2)}) collective-permute-start(f32[128,256]{1,0:T(8,128)S(1)} %get-tuple-element.21), channel_id=1, source_target_pairs={{0,28},{1,29},{2,30},{3,31},{4,8},{5,9},{6,10},{7,11},{8,4},{9,5},... | collective-permute-start | bytes 393224 | tf_op jit(solution)/shard_map/ppermute | solution.py:243
  15.4 18.8 %copy-start.4 = (f32[256,128]{1,0:T(8,128)S(1)}, f32[256,128]{1,0:T(8,128)}, u32[]{:S(2)}) copy-start(f32[256,128]{1,0:T(8,128)} %left.1) | copy-start | bytes 393220
  15.4 18.8 %copy-start.5 = (bf16[2,256,128]{2,1,0:T(8,128)(2,1)S(1)}, bf16[2,256,128]{2,1,0:T(8,128)(2,1)}, u32[]{:S(2)}) copy-start(bf16[2,256,128]{2,1,0:T(8,128)(2,1)} %vectors.1) | copy-start | bytes 393220
  15.4 18.8 %copy-start.6 = (f32[2,128,128]{2,1,0:T(8,128)S(1)}, f32[2,128,128]{2,1,0:T(8,128)}, u32[]{:S(2)}) copy-start(f32[2,128,128]{2,1,0:T(8,128)} %factors.1) | copy-start | bytes 393220
  15.4 19.9 %collective-permute-start.3 = (f32[2,128,256]{2,1,0:T(8,128)S(1)}, f32[2,128,256]{2,1,0:T(8,128)S(1)}, u32[]{:S(2)}, u32[]{:S(2)}) collective-permute-start(f32[2,128,256]{2,1,0:T(8,128)S(1)} %shard_map.83), channel_id=1, source_target_pairs={{0,64},{1,65},{2,66},{3,67},{4,68},{5,69},{6,70},{7,71},{8,72},{9,... | collective-permute-start | bytes 786440 | tf_op jit(solution)/shard_map/ppermute | solution.py:243
  21.4 8.1 %collective-permute-start.2 = (f32[128,256]{1,0:T(8,128)S(1)}, f32[128,256]{1,0:T(8,128)S(1)}, u32[]{:S(2)}, u32[]{:S(2)}) collective-permute-start(f32[128,256]{1,0:T(8,128)S(1)} %get-tuple-element.17), channel_id=1, source_target_pairs={{0,32},{1,33},{2,34},{3,35},{4,36},{5,37},{6,38},{7,39},{8,40},{9,... | collective-permute-start | bytes 393224 | tf_op jit(solution)/shard_map/ppermute | solution.py:243
  23.3 12.0 %copy-start.1 = (bf16[1,1,9,256,256]{4,3,2,1,0:T(8,128)(2,1)S(1)}, bf16[1,1,9,256,256]{4,3,2,1,0:T(8,128)(2,1)}, u32[]{:S(2)}) copy-start(bf16[1,1,9,256,256]{4,3,2,1,0:T(8,128)(2,1)} %node_y.5) | copy-start | bytes 3538948
  23.3 13.3 %collective-permute-start.5 = (f32[2,128,256]{2,1,0:T(8,128)S(1)}, f32[2,128,256]{2,1,0:T(8,128)S(1)}, u32[]{:S(2)}, u32[]{:S(2)}) collective-permute-start(f32[2,128,256]{2,1,0:T(8,128)S(1)} %shard_map.85), channel_id=1, source_target_pairs={{0,4},{1,5},{2,6},{3,7},{4,0},{5,1},{6,2},{7,3},{8,12},{9,13},{10,... | collective-permute-start | bytes 786440 | tf_op jit(solution)/shard_map/ppermute | solution.py:243
  25.4 11.2 %collective-permute-start.6 = (f32[128,256]{1,0:T(8,128)S(1)}, f32[128,256]{1,0:T(8,128)S(1)}, u32[]{:S(2)}, u32[]{:S(2)}) collective-permute-start(f32[128,256]{1,0:T(8,128)S(1)} %get-tuple-element.22), channel_id=1, source_target_pairs={{0,1},{1,0},{2,3},{3,2},{32,33},{33,32},{34,35},{35,34},{64,65},{6... | collective-permute-start | bytes 393224 | tf_op jit(solution)/shard_map/ppermute | solution.py:243
  28.8 7.8 %collective-permute-start.7 = (f32[128,256]{1,0:T(8,128)S(1)}, f32[128,256]{1,0:T(8,128)S(1)}, u32[]{:S(2)}, u32[]{:S(2)}) collective-permute-start(f32[128,256]{1,0:T(8,128)S(1)} %get-tuple-element.22), channel_id=1, source_target_pairs={{4,5},{5,4},{6,7},{7,6},{8,9},{9,8},{10,11},{11,10},{12,13},{13,12... | collective-permute-start | bytes 393224 | tf_op jit(solution)/shard_map/ppermute | solution.py:243
  29.5 8.7 %collective-permute-start.8 = (f32[128,256]{1,0:T(8,128)S(1)}, f32[128,256]{1,0:T(8,128)S(1)}, u32[]{:S(2)}, u32[]{:S(2)}) collective-permute-start(f32[128,256]{1,0:T(8,128)S(1)} %get-tuple-element.26), channel_id=1, source_target_pairs={{0,3},{1,2},{2,1},{3,0},{4,7},{5,6},{6,5},{7,4},{8,11},{9,10},{10,... | collective-permute-start | bytes 393224 | tf_op jit(solution)/shard_map/ppermute | solution.py:243
  36.6 1.7 %copy-start.2 = (bf16[512,256]{1,0:T(8,128)(2,1)S(1)}, bf16[512,256]{1,0:T(8,128)(2,1)}, u32[]{:S(2)}) copy-start(bf16[512,256]{1,0:T(8,128)(2,1)} %leaf_v.1) | copy-start | bytes 786436
  36.6 1.6 %copy-start.3 = (f32[1,1,256,256]{3,2,1,0:T(8,128)S(1)}, f32[1,1,256,256]{3,2,1,0:T(8,128)}, u32[]{:S(2)}) copy-start(f32[1,1,256,256]{3,2,1,0:T(8,128)} %leaf_t.1) | copy-start | bytes 786436
